TPU v7x, 256 devices: a whole 4x4x8 slice. The times are simulated.
256 devices in a mesh: lat: 16 (over x, y_hi, core), lon: 16 (over y_lo, z).
Axes of the slice: x: 4, y: 4 (y_hi: 2, y_lo: 2; y = y_hi * 2 + y_lo), z: 8, core: 2. Of those that a mesh axis runs over, the one named last changes fastest.
Arguments:
- feature: bfloat16 [512, 512, 384], P('lat', 'lon'), may hold values from -6 to 6
- coverage: int32 [512, 512], P('lat', 'lon'), may hold values 0 or 1
- band_rows: int32 [16], replicated, may hold values from 3 to 32, as said below
- depth_weight: bfloat16 [7, 7, 384], replicated, may hold values from -0.875 to 0.875
- norm_gain: float32 [384], replicated, may hold values from 0.25 to 1.75
- norm_shift: float32 [384], replicated, may hold values from -3 to 3
- up_weight: bfloat16 [384, 1536], P('lon'), may hold values from -0.3125 to 0.3125
- up_bias: float32 [1536], replicated, may hold values from -3 to 3
- down_weight: bfloat16 [1536, 384], P('lon'), may hold values from -0.15625 to 0.15625
- down_bias: float32 [384], replicated, may hold values from -3 to 3
- layer_scale: float32 [384], replicated, may hold values from 0.3 to 1.5
- cotangent: bfloat16 [512, 512, 384], P('lat', 'lon'), may hold values from -6 to 6
Outputs:
- block_out: bfloat16 [512, 512, 384], P('lat', 'lon')
- grad_in: bfloat16 [512, 512, 384], P('lat', 'lon')
- grad_up: float32 [384, 1536], P('lon')
- grad_down: float32 [1536, 384], P('lon')
- grad_depth: float32 [7, 7, 384], replicated
Inputs may be any that keep to these rules, and one draw needn't show every extreme that they name: `band_rows`: every band has 3 or more rows, the bands' rows sum to 256, and one band has exactly 32.
All inputs are finite; a program needn't handle non-finite values. No bound on the sum of `coverage` on one device may be relied on, other than what follows from the above.
Results may differ from a plain program's by a relative error of at most 0.0066.
Values may be sent and summed in bfloat16 or wider, within the bound.
A program may use at most 64 MiB of HBM per device.

v0:
```python
import math
import jax
import jax.numpy as jnp
from jax import lax
from jax.sharding import PartitionSpec as P

BAND_MEAN = 16
SQRT_TWO_PI = 0.7978845608028654
CUBIC = 0.044715
EPSILON = 1e-06


def padded(array, sides, width):
    for axis, dim in sides:
        size, length = (lax.axis_size(axis), array.shape[dim])
        up = [(i, (i + 1) % size) for i in range(size)]
        down = [(j, i) for i, j in up]
        last = lax.slice_in_dim(array, length - width, length, axis=dim)
        initial = lax.slice_in_dim(array, 0, width, axis=dim)
        before = lax.ppermute(last, axis, up)
        after = lax.ppermute(initial, axis, down)
        array = jnp.concatenate([before, array, after], axis=dim)
    return array


def shifted(block, axis, distance):
    devices = range(lax.axis_size(axis))
    route = [(i - distance, i) for i in devices if i - distance in devices]
    return lax.ppermute(block, axis, route)


def smooth_gate(pre_act):
    argument = SQRT_TWO_PI * (pre_act + CUBIC * pre_act * pre_act * pre_act)
    return 0.5 * pre_act * (1.0 + jnp.tanh(argument))


def smooth_slope(pre_act):
    argument = SQRT_TWO_PI * (pre_act + CUBIC * pre_act * pre_act * pre_act)
    tangent = jnp.tanh(argument)
    return 0.5 * (1.0 + tangent) + 0.5 * pre_act * (1.0 - tangent * tangent) * SQRT_TWO_PI * (
        1.0 + 3.0 * CUBIC * pre_act * pre_act
    )


def extend(field, live_rows):
    widened = padded(field, (("lon", 1),), 3)
    last_rows = lax.dynamic_slice_in_dim(widened, live_rows - 3, 3, 0)
    from_above = shifted(last_rows, "lat", 1)
    from_below = shifted(widened[:3], "lat", -1)
    zero_rows = jnp.zeros((3,) + widened.shape[1:], widened.dtype)
    stacked = jnp.concatenate([from_above, widened, zero_rows], axis=0)
    return lax.dynamic_update_slice_in_dim(stacked, from_below, live_rows + 3, 0)


def shards(
    feature,
    coverage,
    band_rows,
    depth_weight,
    norm_gain,
    norm_shift,
    up_weight,
    up_bias,
    down_weight,
    down_bias,
    layer_scale,
    cotangent,
):
    rows_max, tile_cols, channels = feature.shape
    kernel = depth_weight.shape[0]
    live_rows = lax.dynamic_index_in_dim(band_rows, lax.axis_index("lat"), 0, keepdims=False)
    inside = jnp.arange(rows_max, dtype=jnp.int32) < live_rows
    covered = jnp.where(inside[:, None], coverage, 0).astype(jnp.bfloat16)
    masked = feature * covered[:, :, None]
    framed = extend(masked, live_rows)
    depth_out = jnp.zeros((rows_max, tile_cols, channels), jnp.float32)
    for row_off in range(kernel):
        for col_off in range(kernel):
            depth_out = depth_out + framed[
                row_off : row_off + rows_max, col_off : col_off + tile_cols
            ].astype(jnp.float32) * depth_weight[row_off, col_off].astype(jnp.float32)
    full_up, full_down = (
        lax.all_gather(up_weight, "lon", axis=0, tiled=True),
        lax.all_gather(down_weight, "lon", axis=0, tiled=True),
    )
    depth_rows = depth_out.reshape(-1, channels)
    center = jnp.mean(depth_rows, axis=-1, keepdims=True)
    offset = depth_rows - center
    scale_inv = lax.rsqrt(jnp.mean(offset * offset, axis=-1, keepdims=True) + EPSILON)
    standard = offset * scale_inv
    normed = (standard * norm_gain + norm_shift).astype(jnp.bfloat16)
    before = jnp.dot(normed, full_up, preferred_element_type=jnp.float32) + up_bias
    active = smooth_gate(before).astype(jnp.bfloat16)
    branch = jnp.dot(active, full_down, preferred_element_type=jnp.float32) + down_bias
    result = (feature.reshape(-1, channels).astype(jnp.float32) + layer_scale * branch).astype(
        jnp.bfloat16
    )
    cot_live = jnp.where(inside[:, None, None], cotangent, jnp.zeros_like(cotangent)).reshape(
        -1, channels
    )
    upstream = (layer_scale * cot_live.astype(jnp.float32)).astype(jnp.bfloat16)
    sum_down = lax.dot_general(
        active, upstream, (((0,), (0,)), ((), ())), preferred_element_type=jnp.float32
    )
    back_active = lax.dot_general(
        upstream, full_down, (((1,), (1,)), ((), ())), preferred_element_type=jnp.float32
    )
    back_before = (back_active * smooth_slope(before)).astype(jnp.bfloat16)
    sum_up = lax.dot_general(
        normed, back_before, (((0,), (0,)), ((), ())), preferred_element_type=jnp.float32
    )
    back_normed = lax.dot_general(
        back_before, full_up, (((1,), (1,)), ((), ())), preferred_element_type=jnp.float32
    )
    back_unit = back_normed * norm_gain
    back_depth = scale_inv * (
        back_unit
        - jnp.mean(back_unit, axis=-1, keepdims=True)
        - standard * jnp.mean(back_unit * standard, axis=-1, keepdims=True)
    )
    back_depth = back_depth.astype(jnp.bfloat16).reshape(rows_max, tile_cols, channels)
    framed_back = extend(back_depth, live_rows)
    spread = jnp.zeros((rows_max, tile_cols, channels), jnp.float32)
    tap_list = []
    for row_off in range(kernel):
        for col_off in range(kernel):
            spread = spread + framed_back[
                6 - row_off : 6 - row_off + rows_max, 6 - col_off : 6 - col_off + tile_cols
            ].astype(jnp.float32) * depth_weight[row_off, col_off].astype(jnp.float32)
            tap_list.append(
                jnp.sum(
                    framed[row_off : row_off + rows_max, col_off : col_off + tile_cols].astype(
                        jnp.float32
                    )
                    * back_depth.astype(jnp.float32),
                    axis=(0, 1),
                )
            )
    grad_local = (
        cotangent.astype(jnp.float32) + covered.astype(jnp.float32)[:, :, None] * spread
    ).astype(jnp.bfloat16)
    grad_in = jnp.where(inside[:, None, None], grad_local, jnp.zeros_like(grad_local))
    block_out = jnp.where(
        inside[:, None, None],
        result.reshape(rows_max, tile_cols, channels),
        jnp.zeros_like(feature),
    )
    rscale = 1.0 / math.sqrt(BAND_MEAN * lax.axis_size("lat") * tile_cols * lax.axis_size("lon"))
    tap_terms = jnp.stack(tap_list, axis=0).reshape(kernel, kernel, channels)
    grad_depth = lax.psum(tap_terms, ("lat", "lon")) * rscale
    up_part, down_part = (
        lax.psum_scatter(sum_up, "lon", scatter_dimension=0, tiled=True),
        lax.psum_scatter(sum_down, "lon", scatter_dimension=0, tiled=True),
    )
    up_part, down_part = lax.psum((up_part, down_part), "lat")
    return (block_out, grad_in, up_part * rscale, down_part * rscale, grad_depth)


def solution(mesh):
    placed = (
        P("lat", "lon", None),
        P("lat", "lon"),
        P(),
        P(),
        P(),
        P(),
        P("lon", None),
        P(),
        P("lon", None),
        P(),
        P(),
        P("lat", "lon", None),
    )
    return jax.shard_map(
        shards,
        mesh=mesh,
        in_specs=placed,
        out_specs=(
            P("lat", "lon", None),
            P("lat", "lon", None),
            P("lon", None),
            P("lon", None),
            P(),
        ),
        check_vma=False,
    )
```

profile of v0, /device:TPU:8, one launch (start us, length us, event | category | flops | bytes accessed | tf_op | source)
XLA Modules:
  0.0 711.5 jit_solution(1951065629706237876)
XLA Ops:
  12.1 2.0 collective-permute-start
  14.1 3.9 collective-permute-start.1
  27.1 3.4 collective-permute-done.3
  30.9 12.5 %fusion.109 = (f32[32,32]{1,0:T(8,128)S(1)}, f32[32,32,384]{2,1,0:T(8,128)S(1)}) fusion(f32[384]{0:T(512)} %get-tuple-element.103, bf16[38,38,384]{2,1,0:T(8,128)(2,1)S(1)} %constant_dynamic-update-slice_fusion.1, f32[384]{0:T(512)} %get-tuple-element.104, f32[384]{0:T(512)S(1)} %get-tuple-element.57, f32[384]{0:T(512)S(1)} %get-tuple-element.58, ...), kind=kLoop, calls=%fused_computation.289 | loop fusion | flops 57801728 | bytes 40187392 | tf_op jit(solution)/shard_map/reduce_sum | solution.py:87
  45.4 36.1 %all-gather.3.cloned.1.call-done = bf16[384,1536]{1,0:T(8,128)(2,1)} async-done(((bf16[24,1536]{1,0:T(8,128)(2,1)}), bf16[384,1536]{1,0:T(8,128)(2,1)}) %all-gather.3.cloned.1.call-update) | async-done | bytes 1179664 | tf_op jit(solution)/shard_map/all_gather | solution.py:83
  81.5 7.8 %multiply_convert_fusion = (bf16[1024,1536]{1,0:T(8,128)(2,1)}, f32[1024,1536]{1,0:T(8,128)}) fusion(f32[1536]{0:T(1024)} %param.19, bf16[1024,384]{1,0:T(8,128)(2,1)} %add_convert_fusion.1, bf16[384,1536]{1,0:T(8,128)(2,1)} %all-gather.3.cloned.1.call-done), kind=kOutput, calls=%fused_computation.58 | convolution fusion | flops 1223688192 | bytes 11409408 | tf_op jit(solution)/shard_map/dot_general | solution.py:92
  89.3 61.2 %all-gather.5.cloned.1.call-done = bf16[1536,384]{1,0:T(8,128)(2,1)} async-done(((bf16[96,384]{1,0:T(8,128)(2,1)}), bf16[1536,384]{1,0:T(8,128)(2,1)}) %all-gather.5.cloned.1.call-update) | async-done | bytes 1179664 | tf_op jit(solution)/shard_map/all_gather | solution.py:84
  150.5 4.2 fusion.105
  157.3 5.4 fusion.6
  162.7 2.0 fusion.107
  164.8 5.0 fusion.103
  169.7 3.0 fusion.67
  172.8 4.0 fusion.85
  178.2 5.2 fusion.116
  184.6 4.7 fusion.115
  190.1 3.5 collective-permute-start.5
  193.6 2.6 collective-permute-done.4
  198.5 218.1 %all-reduce.4.cloned.1.call-done = f32[7,7,384]{2,1,0:T(8,128)} async-done(((f32[7,7,384]{2,1,0:T(8,128)}), f32[7,7,384]{2,1,0:T(8,128)}) %all-reduce.4.cloned.1.call-update) | async-done | bytes 75280 | tf_op jit(solution)/shard_map/psum | solution.py:150
  421.3 68.6 %reduce-scatter.5.cloned.1.call-done = f32[96,384]{1,0:T(8,128)} async-done(((f32[1536,384]{1,0:T(8,128)}), f32[96,384]{1,0:T(8,128)}) %reduce-scatter.5.cloned.1.call-update) | async-done | bytes 147472 | tf_op jit(solution)/shard_map/reduce_scatter | solution.py:153
  489.9 73.4 %reduce-scatter.3.cloned.1.call-done = f32[24,1536]{1,0:T(8,128)} async-done(((f32[384,1536]{1,0:T(8,128)}), f32[24,1536]{1,0:T(8,128)}) %reduce-scatter.3.cloned.1.call-update) | async-done | bytes 147472 | tf_op jit(solution)/shard_map/reduce_scatter | solution.py:152
  563.8 12.6 %broadcast_select_fusion = bf16[32,32,384]{2,1,0:T(8,128)(2,1)} fusion(pred[32]{0:T(512)(128)(4,1)} %copy-done.85, f32[384]{0:T(512)} %get-tuple-element.103, bf16[38,38,384]{2,1,0:T(8,128)(2,1)S(1)} %constant_dynamic-update-slice_fusion, f32[384]{0:T(512)} %get-tuple-element.104, f32[384]{0:T(512)S(1)} %copy-done.46, f32[384]{0:T(512)S(1)} %copy-done.48, ...), kind=kLoop, calls=%fused_computation.221 | loop fusion | flops 59375616 | bytes 40187424 | tf_op jit(solution)/shard_map/jit(_where)/select_n | solution.py:142
  576.3 125.2 %all-reduce.6.cloned.1.call-done = (f32[24,1536]{1,0:T(8,128)}, f32[96,384]{1,0:T(8,128)}) async-done(((f32[24,1536]{1,0:T(8,128)}, f32[96,384]{1,0:T(8,128)}), (f32[24,1536]{1,0:T(8,128)}, f32[96,384]{1,0:T(8,128)})) %all-reduce.6.cloned.1.call-update) | async-done | bytes 294928 | tf_op jit(solution)/shard_map/psum | solution.py:155
  701.5 1.6 broadcast_multiply_fusion.2
  703.1 1.6 broadcast_multiply_fusion.1
  (295 shorter events, 25.4 us)
Async XLA Ops:
  7.2 74.3 %all-gather.3.cloned.1.call-start = ((), (), s32[]{:S(2)}) async-start(), calls=%async_computation.2 | async-start | bytes 1253376 | tf_op jit(solution)/shard_map/all_gather | solution.py:83
  7.9 142.6 %all-gather.5.cloned.1.call-start = ((), (), s32[]{:S(2)}) async-start(), calls=%async_computation.3 | async-start | bytes 1253376 | tf_op jit(solution)/shard_map/all_gather | solution.py:84
  12.1 9.8 %collective-permute-start = (bf16[32,3,384]{2,1,0:T(4,128)(2,1)S(1)}, bf16[32,3,384]{2,1,0:T(4,128)(2,1)S(1)}, u32[]{:S(2)}, u32[]{:S(2)}) collective-permute-start(bf16[32,3,384]{2,1,0:T(4,128)(2,1)S(1)} %get-tuple-element.118), channel_id=1, source_target_pairs={{0,1},{1,2},{2,3},{3,4},{4,5},{5,6},{6,7},{7,8},{8,9},{9,10},{10,1... | collective-permute-start | bytes 221192 | tf_op jit(solution)/shard_map/ppermute | solution.py:20
  14.1 7.9 %collective-permute-start.1 = (bf16[32,3,384]{2,1,0:T(4,128)(2,1)S(1)}, bf16[32,3,384]{2,1,0:T(4,128)(2,1)S(1)}, u32[]{:S(2)}, u32[]{:S(2)}) collective-permute-start(bf16[32,3,384]{2,1,0:T(4,128)(2,1)S(1)} %get-tuple-element.119), channel_id=1, source_target_pairs={{1,0},{2,1},{3,2},{4,3},{5,4},{6,5},{7,6},{8,7},{9,8},{10,9},{11,1... | collective-permute-start | bytes 221192 | tf_op jit(solution)/shard_map/ppermute | solution.py:21
  18.0 398.6 %all-reduce.4.cloned.1.call-start = ((), (), s32[]{:S(2)}) async-start(), calls=%async_computation.6 | async-start | bytes 172032 | tf_op jit(solution)/shard_map/psum | solution.py:150
  22.6 3.4 collective-permute-start.2
  24.7 5.8 collective-permute-start.3
  178.2 311.8 %reduce-scatter.5.cloned.1.call-start = ((), (), s32[]{:S(2)}) async-start(), calls=%async_computation.5 | async-start | bytes 2506752 | tf_op jit(solution)/shard_map/reduce_scatter | solution.py:153
  183.4 379.9 %reduce-scatter.3.cloned.1.call-start = ((), (), s32[]{:S(2)}) async-start(), calls=%async_computation.4 | async-start | bytes 2506752 | tf_op jit(solution)/shard_map/reduce_scatter | solution.py:152
  189.3 512.2 %all-reduce.6.cloned.1.call-start = ((), (), s32[]{:S(2)}) async-start(), calls=%async_computation.7 | async-start | bytes 589824 | tf_op jit(solution)/shard_map/psum | solution.py:155
  189.4 6.8 collective-permute-start.4
  190.1 6.1 collective-permute-start.5
  196.8 366.5 %copy-start.1 = (bf16[32,32,384]{2,1,0:T(8,128)(2,1)S(1)}, bf16[32,32,384]{2,1,0:T(8,128)(2,1)}, u32[]{:S(2)}) copy-start(bf16[32,32,384]{2,1,0:T(8,128)(2,1)} %param.23) | copy-start | bytes 2359300
  196.8 366.5 %copy-start.8 = (f32[384]{0:T(512)S(1)}, f32[384]{0:T(512)}, u32[]{:S(2)}) copy-start(f32[384]{0:T(512)} %copy-done.7) | copy-start | bytes 4612
  196.8 366.5 %copy-start.10 = (f32[384]{0:T(512)S(1)}, f32[384]{0:T(512)}, u32[]{:S(2)}) copy-start(f32[384]{0:T(512)} %copy-done.9) | copy-start | bytes 4612
  196.8 366.5 %copy-start.12 = (f32[384]{0:T(512)S(1)}, f32[384]{0:T(512)}, u32[]{:S(2)}) copy-start(f32[384]{0:T(512)} %copy-done.11) | copy-start | bytes 4612
  196.9 366.5 %copy-start.14 = (f32[384]{0:T(512)S(1)}, f32[384]{0:T(512)}, u32[]{:S(2)}) copy-start(f32[384]{0:T(512)} %copy-done.13) | copy-start | bytes 4612
  196.9 366.5 %copy-start.16 = (f32[384]{0:T(512)S(1)}, f32[384]{0:T(512)}, u32[]{:S(2)}) copy-start(f32[384]{0:T(512)} %copy-done.15) | copy-start | bytes 4612
  196.9 366.5 %copy-start.18 = (f32[384]{0:T(512)S(1)}, f32[384]{0:T(512)}, u32[]{:S(2)}) copy-start(f32[384]{0:T(512)} %copy-done.17) | copy-start | bytes 4612
  196.9 366.5 %copy-start.20 = (f32[384]{0:T(512)S(1)}, f32[384]{0:T(512)}, u32[]{:S(2)}) copy-start(f32[384]{0:T(512)} %copy-done.19) | copy-start | bytes 4612
  196.9 366.5 %copy-start.22 = (f32[384]{0:T(512)S(1)}, f32[384]{0:T(512)}, u32[]{:S(2)}) copy-start(f32[384]{0:T(512)} %copy-done.21) | copy-start | bytes 4612
  196.9 366.5 %copy-start.24 = (f32[384]{0:T(512)S(1)}, f32[384]{0:T(512)}, u32[]{:S(2)}) copy-start(f32[384]{0:T(512)} %copy-done.23) | copy-start | bytes 4612
  197.2 222.2 %collective-permute-start.6 = (bf16[3,38,384]{2,1,0:T(8,128)(2,1)S(1)}, bf16[3,38,384]{2,1,0:T(8,128)(2,1)S(1)}, u32[]{:S(2)}, u32[]{:S(2)}) collective-permute-start(bf16[3,38,384]{2,1,0:T(8,128)(2,1)S(1)} %get-tuple-element.113), channel_id=1, source_target_pairs={{0,16},{16,32},{32,48},{48,64},{64,80},{80,96},{96,112},{112,128},... | collective-permute-start | bytes 262664 | tf_op jit(solution)/shard_map/ppermute | solution.py:29
  418.1 3.2 collective-permute-start.7
  (86 other events, 11544.8 us)
Sparse Core Ops, SparseCore 0:
  9.8 71.6 all-gather.2
  83.3 67.1 all-gather.4
  178.3 238.2 all-reduce.3
  419.0 70.8 reduce-scatter.4
  492.3 70.9 reduce-scatter.2
  565.9 135.5 all-reduce.5
where the time goes:
time: 712 us
  waiting for transfers between devices  590 us (83%)
  other arithmetic  51.7 us (7%)
  matrix products  29.3 us (4%)
  between operations  18.7 us (3%)
  starting transfers between devices  15.7 us (2%)
    psum x1, waiting for transfers between devices, shards(): grad_depth = lax.psum(tap_terms, ('lat', 'lon')) * rscale  218 us
    psum x1, waiting for transfers between devices, shards(): up_part, down_part = lax.psum((up_part, down_part), 'lat')  125 us
    reduce_scatter x1, waiting for transfers between devices, shards(): lax.psum_scatter(sum_up, 'lon', scatter_dimension=0, tiled=True)  73.4 us
    reduce_scatter x1, waiting for transfers between devices, shards(): lax.psum_scatter(sum_down, 'lon', scatter_dimension=0, tiled=True)  68.6 us
    all_gather x1, waiting for transfers between devices, shards(): lax.all_gather(down_weight, 'lon', axis=0, tiled=True)  61.2 us
    all_gather x1, waiting for transfers between devices, shards(): lax.all_gather(up_weight, 'lon', axis=0, tiled=True)  36.1 us
  transfers between devices with their start and end apart: 14, of which 9 were waited for; matrix products, arithmetic and copies ran while one was open for 8% of the time, Pallas kernels for 0%

commit v1 on v0

--- a/solution.py
+++ b/solution.py
@@ -8,6 +8,11 @@
 SQRT_TWO_PI = 0.7978845608028654
 CUBIC = 0.044715
 EPSILON = 1e-06
+
+
+def axis_by_axis(array_2, axis_one, axis_two):
+    inner = lax.psum(array_2, axis_one)
+    return lax.psum(inner, axis_two)
 
 
 def padded(array, sides, width):
@@ -147,7 +152,7 @@
     )
     rscale = 1.0 / math.sqrt(BAND_MEAN * lax.axis_size("lat") * tile_cols * lax.axis_size("lon"))
     tap_terms = jnp.stack(tap_list, axis=0).reshape(kernel, kernel, channels)
-    grad_depth = lax.psum(tap_terms, ("lat", "lon")) * rscale
+    grad_depth = axis_by_axis(tap_terms, "lat", "lon") * rscale
     up_part, down_part = (
         lax.psum_scatter(sum_up, "lon", scatter_dimension=0, tiled=True),
         lax.psum_scatter(sum_down, "lon", scatter_dimension=0, tiled=True),

time: 712 us -> 592 us (0.83)
  waiting for transfers between devices: 590 us -> 470 us
    psum x1, waiting for transfers between devices: 218 us -> 129 us  [axis_by_axis(): return lax.psum(inner, axis_two)]
    reduce_scatter x1, waiting for transfers between devices: 68.6 us -> 30.6 us  [shards(): lax.psum_scatter(sum_down, 'lon', scatter_dimension=0, tiled=True)]
  transfers between devices with their start and end apart: 14 -> 14, of which waited for: 9 -> 8; matrix products, arithmetic and copies ran while one was open for 8% -> 12% of each run, Pallas kernels for 0% -> 0%
where the time goes in v1:
time: 592 us; the launch traced here: 591 us
  waiting for transfers between devices  470 us (79%)
  other arithmetic  49.5 us (8%)
  matrix products  29.4 us (5%)
  between operations  18.8 us (3%)
  starting transfers between devices  16.4 us (3%)
  local copies, waits for them, and re-layouts  6.35 us (1%)
    psum x1, waiting for transfers between devices, shards(): up_part, down_part = lax.psum((up_part, down_part), 'lat')  131 us
    psum x1, waiting for transfers between devices, axis_by_axis(): return lax.psum(inner, axis_two)  129 us
    reduce_scatter x1, waiting for transfers between devices, shards(): lax.psum_scatter(sum_up, 'lon', scatter_dimension=0, tiled=True)  73.5 us
    all_gather x1, waiting for transfers between devices, shards(): lax.all_gather(down_weight, 'lon', axis=0, tiled=True)  61.2 us
    all_gather x1, waiting for transfers between devices, shards(): lax.all_gather(up_weight, 'lon', axis=0, tiled=True)  37.6 us
    reduce_scatter x1, waiting for transfers between devices, shards(): lax.psum_scatter(sum_down, 'lon', scatter_dimension=0, tiled=True)  30.6 us
    select_n x1, other arithmetic, shards(): jnp.where(inside[:, None, None], grad_local, jnp.zeros_like(grad_local))  12.3 us
  transfers between devices with their start and end apart: 14, of which 8 were waited for; matrix products, arithmetic and copies ran while one was open for 12% of the time, Pallas kernels for 0%

profile of v1, /device:TPU:8, one launch (start us, length us, event | category | flops | bytes accessed | tf_op | source)
XLA Modules:
  0.0 590.6 jit_solution(18299306006039303611)
XLA Ops:
  12.1 2.0 collective-permute-start
  14.1 3.9 collective-permute-start.1
  26.1 3.9 collective-permute-done.3
  30.4 11.6 %fusion.109 = (f32[32,32]{1,0:T(8,128)S(1)}, f32[32,32,384]{2,1,0:T(8,128)S(1)}) fusion(f32[384]{0:T(512)S(1)} %get-tuple-element.103, bf16[38,38,384]{2,1,0:T(8,128)(2,1)S(1)} %constant_dynamic-update-slice_fusion.1, f32[384]{0:T(512)S(1)} %get-tuple-element.104, f32[384]{0:T(512)S(1)} %get-tuple-element.57, f32[384]{0:T(512)S(1)} %get-tuple-element.58, ...), kind=kLoop, calls=%fused_computation.289 | loop fusion | flops 57801728 | bytes 40187392 | tf_op jit(solution)/shard_map/reduce_sum | solution.py:92
  44.0 37.6 %all-gather.3.cloned.1.call-done = bf16[384,1536]{1,0:T(8,128)(2,1)} async-done(((bf16[24,1536]{1,0:T(8,128)(2,1)}), bf16[384,1536]{1,0:T(8,128)(2,1)}) %all-gather.3.cloned.1.call-update) | async-done | bytes 1179664 | tf_op jit(solution)/shard_map/all_gather | solution.py:88
  81.6 7.8 %multiply_convert_fusion = (bf16[1024,1536]{1,0:T(8,128)(2,1)}, f32[1024,1536]{1,0:T(8,128)}) fusion(f32[1536]{0:T(1024)} %param.19, bf16[1024,384]{1,0:T(8,128)(2,1)} %add_convert_fusion.1, bf16[384,1536]{1,0:T(8,128)(2,1)} %all-gather.3.cloned.1.call-done), kind=kOutput, calls=%fused_computation.58 | convolution fusion | flops 1223688192 | bytes 11409408 | tf_op jit(solution)/shard_map/dot_general | solution.py:97
  89.4 61.2 %all-gather.5.cloned.1.call-done = bf16[1536,384]{1,0:T(8,128)(2,1)} async-done(((bf16[96,384]{1,0:T(8,128)(2,1)}), bf16[1536,384]{1,0:T(8,128)(2,1)}) %all-gather.5.cloned.1.call-update) | async-done | bytes 1179664 | tf_op jit(solution)/shard_map/all_gather | solution.py:89
  150.6 4.1 fusion.105
  156.9 3.3 fusion.116
  160.5 7.1 %fusion.6 = bf16[1024,1536]{1,0:T(8,128)(2,1)S(1)} fusion(f32[1024,1536]{1,0:T(8,128)} %get-tuple-element.124, bf16[1024,384]{1,0:T(8,128)(2,1)S(1)} %fusion.104, bf16[1536,384]{1,0:T(8,128)(2,1)} %all-gather.5.cloned.1.call-done, f32[1536]{0:T(1024)} %param.19), kind=kOutput, calls=%fused_computation.57 | convolution fusion | flops 1239416832 | bytes 11409408 | tf_op jit(solution)/shard_map/dot_general | solution.py:110
  167.7 1.7 copy-done.99
  169.3 2.9 fusion.115
  172.8 4.2 fusion.107
  177.0 5.0 fusion.103
  182.8 3.5 collective-permute-start.5
  186.3 3.9 fusion.85
  192.2 2.8 fusion.67
  199.4 3.1 collective-permute-done.7
  202.5 30.6 %reduce-scatter.5.cloned.1.call-done = f32[96,384]{1,0:T(8,128)} async-done(((f32[1536,384]{1,0:T(8,128)}), f32[96,384]{1,0:T(8,128)}) %reduce-scatter.5.cloned.1.call-update) | async-done | bytes 147472 | tf_op jit(solution)/shard_map/reduce_scatter | solution.py:158
  233.1 73.5 %reduce-scatter.3.cloned.1.call-done = f32[24,1536]{1,0:T(8,128)} async-done(((f32[384,1536]{1,0:T(8,128)}), f32[24,1536]{1,0:T(8,128)}) %reduce-scatter.3.cloned.1.call-update) | async-done | bytes 147472 | tf_op jit(solution)/shard_map/reduce_scatter | solution.py:157
  307.0 12.3 %broadcast_select_fusion = bf16[32,32,384]{2,1,0:T(8,128)(2,1)} fusion(pred[32]{0:T(512)(128)(4,1)} %copy-done.92, f32[384]{0:T(512)} %copy-done.90, bf16[38,38,384]{2,1,0:T(8,128)(2,1)S(1)} %constant_dynamic-update-slice_fusion, f32[384]{0:T(512)} %copy-done.91, f32[384]{0:T(512)S(1)} %copy-done.44, f32[384]{0:T(512)S(1)} %copy-done.46, ...), kind=kLoop, calls=%fused_computation.221 | loop fusion | flops 59375616 | bytes 40187424 | tf_op jit(solution)/shard_map/jit(_where)/select_n | solution.py:147
  319.4 130.9 %all-reduce.6.cloned.1.call-done = (f32[24,1536]{1,0:T(8,128)}, f32[96,384]{1,0:T(8,128)}, f32[7,7,384]{2,1,0:T(8,128)}) async-done(((f32[24,1536]{1,0:T(8,128)}, f32[96,384]{1,0:T(8,128)}, f32[7,7,384]{2,1,0:T(8,128)}), (f32[24,1536]{1,0:T(8,128)}, f32[96,384]{1,0:T(8,128)}, f32[7,7,384]{2,1,0:T(8,128)})) %all-reduce.6.cloned.1.call-update) | async-done | bytes 370192 | tf_op jit(solution)/shard_map/psum | solution.py:160
  451.9 1.6 broadcast_multiply_fusion.1
  453.4 128.8 %all-reduce.4.cloned.1.call-done = f32[7,7,384]{2,1,0:T(8,128)} async-done(((f32[7,7,384]{2,1,0:T(8,128)}), f32[7,7,384]{2,1,0:T(8,128)}) %all-reduce.4.cloned.1.call-update) | async-done | bytes 75280 | tf_op jit(solution)/shard_map/psum | solution.py:15
  (305 shorter events, 24.8 us)
Async XLA Ops:
  7.2 74.4 %all-gather.3.cloned.1.call-start = ((), (), s32[]{:S(2)}) async-start(), calls=%async_computation.2 | async-start | bytes 1253376 | tf_op jit(solution)/shard_map/all_gather | solution.py:88
  7.9 142.7 %all-gather.5.cloned.1.call-start = ((), (), s32[]{:S(2)}) async-start(), calls=%async_computation.3 | async-start | bytes 1253376 | tf_op jit(solution)/shard_map/all_gather | solution.py:89
  12.1 9.7 %collective-permute-start = (bf16[32,3,384]{2,1,0:T(4,128)(2,1)S(1)}, bf16[32,3,384]{2,1,0:T(4,128)(2,1)S(1)}, u32[]{:S(2)}, u32[]{:S(2)}) collective-permute-start(bf16[32,3,384]{2,1,0:T(4,128)(2,1)S(1)} %get-tuple-element.119), channel_id=1, source_target_pairs={{0,1},{1,2},{2,3},{3,4},{4,5},{5,6},{6,7},{7,8},{8,9},{9,10},{10,1... | collective-permute-start | bytes 221192 | tf_op jit(solution)/shard_map/ppermute | solution.py:25
  14.1 7.7 %collective-permute-start.1 = (bf16[32,3,384]{2,1,0:T(4,128)(2,1)S(1)}, bf16[32,3,384]{2,1,0:T(4,128)(2,1)S(1)}, u32[]{:S(2)}, u32[]{:S(2)}) collective-permute-start(bf16[32,3,384]{2,1,0:T(4,128)(2,1)S(1)} %get-tuple-element.120), channel_id=1, source_target_pairs={{1,0},{2,1},{3,2},{4,3},{5,4},{6,5},{7,6},{8,7},{9,8},{10,9},{11,1... | collective-permute-start | bytes 221192 | tf_op jit(solution)/shard_map/ppermute | solution.py:26
  18.0 215.1 %reduce-scatter.5.cloned.1.call-start = ((), (), s32[]{:S(2)}) async-start(), calls=%async_computation.5 | async-start | bytes 2506752 | tf_op jit(solution)/shard_map/reduce_scatter | solution.py:158
  22.5 3.1 collective-permute-start.2
  24.2 5.8 collective-permute-start.3
  160.2 146.3 %reduce-scatter.3.cloned.1.call-start = ((), (), s32[]{:S(2)}) async-start(), calls=%async_computation.4 | async-start | bytes 2506752 | tf_op jit(solution)/shard_map/reduce_scatter | solution.py:157
  172.2 278.1 %all-reduce.6.cloned.1.call-start = ((), (), s32[]{:S(2)}) async-start(), calls=%async_computation.7 | async-start | bytes 761856 | tf_op jit(solution)/shard_map/psum | solution.py:160
  182.1 8.1 %collective-permute-start.4 = (bf16[32,3,384]{2,1,0:T(4,128)(2,1)S(1)}, bf16[32,3,384]{2,1,0:T(4,128)(2,1)S(1)}, u32[]{:S(2)}, u32[]{:S(2)}) collective-permute-start(bf16[32,3,384]{2,1,0:T(4,128)(2,1)S(1)} %get-tuple-element.117), channel_id=1, source_target_pairs={{0,1},{1,2},{2,3},{3,4},{4,5},{5,6},{6,7},{7,8},{8,9},{9,10},{10,1... | collective-permute-start | bytes 221192 | tf_op jit(solution)/shard_map/ppermute | solution.py:25
  182.8 7.4 %collective-permute-start.5 = (bf16[32,3,384]{2,1,0:T(4,128)(2,1)S(1)}, bf16[32,3,384]{2,1,0:T(4,128)(2,1)S(1)}, u32[]{:S(2)}, u32[]{:S(2)}) collective-permute-start(bf16[32,3,384]{2,1,0:T(4,128)(2,1)S(1)} %get-tuple-element.118), channel_id=1, source_target_pairs={{1,0},{2,1},{3,2},{4,3},{5,4},{6,5},{7,6},{8,7},{9,8},{10,9},{11,1... | collective-permute-start | bytes 221192 | tf_op jit(solution)/shard_map/ppermute | solution.py:26
  190.8 7.5 %collective-permute-start.6 = (bf16[3,38,384]{2,1,0:T(8,128)(2,1)S(1)}, bf16[3,38,384]{2,1,0:T(8,128)(2,1)S(1)}, u32[]{:S(2)}, u32[]{:S(2)}) collective-permute-start(bf16[3,38,384]{2,1,0:T(8,128)(2,1)S(1)} %get-tuple-element.114), channel_id=1, source_target_pairs={{0,16},{16,32},{32,48},{48,64},{64,80},{80,96},{96,112},{112,128},... | collective-permute-start | bytes 262664 | tf_op jit(solution)/shard_map/ppermute | solution.py:34
  195.5 111.1 %copy-start.1 = (bf16[32,32,384]{2,1,0:T(8,128)(2,1)S(1)}, bf16[32,32,384]{2,1,0:T(8,128)(2,1)}, u32[]{:S(2)}) copy-start(bf16[32,32,384]{2,1,0:T(8,128)(2,1)} %param.23) | copy-start | bytes 2359300
  195.5 111.1 %copy-start.6 = (f32[384]{0:T(512)S(1)}, f32[384]{0:T(512)}, u32[]{:S(2)}) copy-start(f32[384]{0:T(512)} %copy-done.5) | copy-start | bytes 4612
  195.5 111.1 %copy-start.8 = (f32[384]{0:T(512)S(1)}, f32[384]{0:T(512)}, u32[]{:S(2)}) copy-start(f32[384]{0:T(512)} %copy-done.7) | copy-start | bytes 4612
  195.5 111.1 %copy-start.10 = (f32[384]{0:T(512)S(1)}, f32[384]{0:T(512)}, u32[]{:S(2)}) copy-start(f32[384]{0:T(512)} %get-tuple-element.78) | copy-start | bytes 4612
  195.5 111.1 %copy-start.12 = (f32[384]{0:T(512)S(1)}, f32[384]{0:T(512)}, u32[]{:S(2)}) copy-start(f32[384]{0:T(512)} %get-tuple-element.79) | copy-start | bytes 4612
  195.6 111.1 %copy-start.14 = (f32[384]{0:T(512)S(1)}, f32[384]{0:T(512)}, u32[]{:S(2)}) copy-start(f32[384]{0:T(512)} %get-tuple-element.80) | copy-start | bytes 4612
  195.6 111.1 %copy-start.16 = (f32[384]{0:T(512)S(1)}, f32[384]{0:T(512)}, u32[]{:S(2)}) copy-start(f32[384]{0:T(512)} %get-tuple-element.81) | copy-start | bytes 4612
  195.6 111.1 %copy-start.18 = (f32[384]{0:T(512)S(1)}, f32[384]{0:T(512)}, u32[]{:S(2)}) copy-start(f32[384]{0:T(512)} %get-tuple-element.82) | copy-start | bytes 4612
  195.6 111.1 %copy-start.20 = (f32[384]{0:T(512)S(1)}, f32[384]{0:T(512)}, u32[]{:S(2)}) copy-start(f32[384]{0:T(512)} %get-tuple-element.83) | copy-start | bytes 4612
  195.6 111.1 %copy-start.22 = (f32[384]{0:T(512)S(1)}, f32[384]{0:T(512)}, u32[]{:S(2)}) copy-start(f32[384]{0:T(512)} %get-tuple-element.84) | copy-start | bytes 4612
  196.8 5.7 collective-permute-start.7
  306.6 275.6 %all-reduce.4.cloned.1.call-start = ((), (), s32[]{:S(2)}) async-start(), calls=%async_computation.6 | async-start | bytes 172032 | tf_op jit(solution)/shard_map/psum | solution.py:15
  (91 other events, 3985.4 us)
Sparse Core Ops, SparseCore 0:
  9.8 71.7 all-gather.2
  83.4 67.1 all-gather.4
  160.3 72.7 reduce-scatter.4
  235.5 71.0 reduce-scatter.2
  309.8 140.3 all-reduce.5
  452.9 129.2 all-reduce.3
